TPU v7x, 32 devices: a whole 2x2x4 slice. The times are simulated.
32 devices in a mesh: dp: 8 (over z, x), seq: 4 (over y, core).
Axes of the slice: x: 2, y: 2, z: 4, core: 2. Of those that a mesh axis runs over, the one named last changes fastest.
Arguments:
- tokens: bfloat16 [2, 8, 1024, 2048], P(None, 'dp', 'seq'), may hold values from -6 to 6
- lengths: int32 [2, 8], P(None, 'dp'), may hold values from 256 to 1024, as said below
- cotangent: bfloat16 [2, 8, 1024, 2048], P(None, 'dp', 'seq'), may hold values from -6 to 6
- norm_gain: bfloat16 [2048], P(('dp', 'seq')), may hold values from 0.099609375 to 1.8984375
- in_weight: bfloat16 [2048, 8192], P(('dp', 'seq')), may hold values from -0.125 to 0.125
- conv_weight: bfloat16 [4, 4096], P(None, ('dp', 'seq')), may hold values from -3 to 3
- conv_bias: bfloat16 [4096], P(('dp', 'seq')), may hold values from -3 to 3
- x_weight: bfloat16 [4096, 160], P(('dp', 'seq')), may hold values from -0.09375 to 0.09375
- dt_weight: bfloat16 [128, 4096], P(None, ('dp', 'seq')), may hold values from -0.5 to 0.5
- dt_bias: bfloat16 [4096], P(('dp', 'seq')), may hold values from -8 to -2
- a_log: bfloat16 [16, 4096], P(None, ('dp', 'seq')), may hold values from -2 to 2.765625
- skip_d: bfloat16 [4096], P(('dp', 'seq')), may hold values from 0.5 to 2
- out_weight: bfloat16 [4096, 2048], P(('dp', 'seq')), may hold values from -0.25 to 0.25
Outputs:
- block_out: bfloat16 [2, 8, 1024, 2048], P(None, 'dp', 'seq')
- input_grad: bfloat16 [2, 8, 1024, 2048], P(None, 'dp', 'seq')
- grad_norm_gain: float32 [2048], P(('dp', 'seq'))
- grad_in_weight: float32 [2048, 8192], P(('dp', 'seq'))
- grad_conv_weight: float32 [4, 4096], P(None, ('dp', 'seq'))
- grad_conv_bias: float32 [4096], P(('dp', 'seq'))
- grad_x_weight: float32 [4096, 160], P(('dp', 'seq'))
- grad_dt_weight: float32 [128, 4096], P(None, ('dp', 'seq'))
- grad_dt_bias: float32 [4096], P(('dp', 'seq'))
- grad_a_log: float32 [16, 4096], P(None, ('dp', 'seq'))
- grad_skip_d: float32 [4096], P(('dp', 'seq'))
- grad_out_weight: float32 [4096, 2048], P(('dp', 'seq'))
Inputs may be any that keep to these rules, and one draw needn't show every extreme that they name: `lengths`: the number of leading positions of each slot that hold tokens; later positions are padding.
All inputs are finite; a program needn't handle non-finite values.
Results may differ from a plain program's by a relative error of at most 0.012.
Values may be sent and summed in bfloat16 or wider, within the bound.
No kernel may reach another device: no remote copies, remote signals or barrier semaphores. Data moves between devices by JAX's collectives and lax.ppermute only.
A program may use at most 320 MiB of HBM per device.

v0:
```python
import jax
import jax.numpy as jnp
from jax import lax
from jax.sharding import PartitionSpec as P

KCONV = 4
BLOCK = 16


EPSILON = 1e-05


def shifted(value, axis, steps):
    count = lax.axis_size(axis)
    initial, last = (max(0, -steps), min(count, count - steps))
    return lax.ppermute(value, axis, [(source, source + steps) for source in range(initial, last)])


def prefix(shard, axis, combine, identity):
    peers, index = (lax.axis_size(axis), lax.axis_index(axis))
    everything = jax.tree.map(
        lambda part, kind: lax.all_gather(part.astype(kind), axis),
        shard,
        (jnp.bfloat16, jnp.bfloat16),
    )
    start = jax.tree.map(
        lambda part, zero: jnp.broadcast_to(jnp.asarray(zero, part.dtype), part.shape),
        shard,
        identity,
    )

    def prefix_lap(k, before):
        reached = k < index
        new = combine(
            before, jax.tree.map(lambda part, own: part[k].astype(own.dtype), everything, shard)
        )
        return jax.tree.map(lambda a, b: jnp.where(reached, a, b), new, before)

    return lax.fori_loop(0, peers, prefix_lap, start)


def entering(shard, axis, combine, identity):
    peers, index = (lax.axis_size(axis), lax.axis_index(axis))
    everything = jax.tree.map(lambda part: lax.all_gather(part, axis), shard)
    start = jax.tree.map(
        lambda part, zero: jnp.broadcast_to(jnp.asarray(zero, part.dtype), part.shape),
        shard,
        identity,
    )

    def entering_lap(k, before):
        at = peers - 1 - k
        reached = at > index
        new = combine(before, jax.tree.map(lambda part: part[at], everything))
        return jax.tree.map(lambda a, b: jnp.where(reached, a, b), new, before)

    return lax.fori_loop(0, peers, entering_lap, start)


def for_sending(shard):
    return jax.tree.map(lambda a: a.astype(jnp.bfloat16) if a.dtype == jnp.float32 else a, shard)


def affine_join(earlier, later):
    return (earlier[0] * later[0], later[0] * earlier[1] + later[1])


def blocks_of(array):
    slots, length = (array.shape[0], array.shape[1])
    shaped = array.reshape((slots, length // BLOCK, BLOCK) + array.shape[2:])
    return jnp.moveaxis(shaped, 1, 0)


def unblock(array):
    moved = jnp.moveaxis(array, 0, 1)
    return moved.reshape((moved.shape[0], moved.shape[1] * moved.shape[2]) + moved.shape[3:])


def gather_forward(shards):
    gain, input_projection, w_conv, b_conv, w_x, w_dt, b_dt, a_log, skip, output_projection = shards
    return (
        lax.all_gather(gain, ("dp", "seq"), axis=0, tiled=True),
        lax.all_gather(input_projection, ("dp", "seq"), axis=0, tiled=True),
        lax.all_gather(w_conv, ("dp", "seq"), axis=1, tiled=True),
        lax.all_gather(b_conv, ("dp", "seq"), axis=0, tiled=True),
        lax.all_gather(w_x, ("dp", "seq"), axis=0, tiled=True),
        lax.all_gather(w_dt, ("dp", "seq"), axis=1, tiled=True),
        lax.all_gather(b_dt, ("dp", "seq"), axis=0, tiled=True),
        lax.all_gather(a_log, ("dp", "seq"), axis=1, tiled=True),
        lax.all_gather(skip, ("dp", "seq"), axis=0, tiled=True),
        lax.all_gather(output_projection, ("dp", "seq"), axis=0, tiled=True),
    )


def gather_backward(shards):
    gain, input_projection, w_conv, b_conv, w_x, w_dt, b_dt, a_log, skip, output_projection = shards
    return (
        lax.all_gather(gain, ("dp", "seq"), axis=0, tiled=True),
        lax.all_gather(input_projection, ("dp", "seq"), axis=0, tiled=True),
        lax.all_gather(w_conv, ("dp", "seq"), axis=1, tiled=True),
        lax.all_gather(b_conv, ("dp", "seq"), axis=0, tiled=True),
        lax.all_gather(w_x, ("dp", "seq"), axis=0, tiled=True),
        lax.all_gather(w_dt, ("dp", "seq"), axis=1, tiled=True),
        lax.all_gather(b_dt, ("dp", "seq"), axis=0, tiled=True),
        lax.all_gather(a_log, ("dp", "seq"), axis=1, tiled=True),
        lax.all_gather(skip, ("dp", "seq"), axis=0, tiled=True),
        lax.all_gather(output_projection, ("dp", "seq"), axis=0, tiled=True),
    )


def scatter_each(grads):
    g_gain, g_in, g_conv, g_bconv, g_x, g_dt, g_bdt, g_alog, g_skip, g_out = grads
    return (
        lax.psum_scatter(g_gain, ("dp", "seq"), scatter_dimension=0, tiled=True),
        lax.psum_scatter(g_in, ("dp", "seq"), scatter_dimension=0, tiled=True),
        lax.psum_scatter(g_conv, ("dp", "seq"), scatter_dimension=1, tiled=True),
        lax.psum_scatter(g_bconv, ("dp", "seq"), scatter_dimension=0, tiled=True),
        lax.psum_scatter(g_x, ("dp", "seq"), scatter_dimension=0, tiled=True),
        lax.psum_scatter(g_dt, ("dp", "seq"), scatter_dimension=1, tiled=True),
        lax.psum_scatter(g_bdt, ("dp", "seq"), scatter_dimension=0, tiled=True),
        lax.psum_scatter(g_alog, ("dp", "seq"), scatter_dimension=1, tiled=True),
        lax.psum_scatter(g_skip, ("dp", "seq"), scatter_dimension=0, tiled=True),
        lax.psum_scatter(g_out, ("dp", "seq"), scatter_dimension=0, tiled=True),
    )


def weighted_total(exponent, left, right, decay_rate):

    def add_block(total, pieces):
        power, left_blk, right_blk = pieces
        term = (
            jnp.exp(power[:, :, None, :] * decay_rate[None, None])
            * left_blk[..., None]
            * right_blk[:, :, None, :]
        )
        return (total + jnp.sum(term, axis=1), None)

    initial = jnp.zeros((exponent.shape[0],) + decay_rate.shape, jnp.float32)
    total, unused = lax.scan(
        add_block, initial, (blocks_of(exponent), blocks_of(left), blocks_of(right))
    )
    return total


def run_forward(state_in, step_size, b_in, c_out, conv_f, decay_rate):

    def advance(state, pieces):
        steps, b_blk, c_blk, x_blk = pieces
        first = state
        outputs = []
        for index in range(BLOCK):
            factor = jnp.exp(steps[:, index, None, :] * decay_rate[None])
            state = (
                factor * state
                + b_blk[:, index, :, None] * (steps[:, index] * x_blk[:, index])[:, None, :]
            )
            outputs.append(jnp.sum(c_blk[:, index, :, None] * state, axis=1))
        return (state, (jnp.stack(outputs, axis=1), first))

    final, (outputs, starts) = lax.scan(
        advance,
        state_in,
        (blocks_of(step_size), blocks_of(b_in), blocks_of(c_out), blocks_of(conv_f)),
    )
    return (unblock(outputs), starts)


def run_backward(adjoint_in, starts, step_size, b_in, c_out, conv_f, scan_grad, decay_rate):

    def retreat(carry, pieces):
        adjoint, decay_grad = carry
        start_state, steps, b_blk, c_blk, x_blk, y_blk = pieces
        history = [start_state]
        factors = []
        drives = []
        state = start_state
        for index in range(BLOCK):
            factor = jnp.exp(steps[:, index, None, :] * decay_rate[None])
            drive = steps[:, index] * x_blk[:, index]
            state = factor * state + b_blk[:, index, :, None] * drive[:, None, :]
            history.append(state)
            factors.append(factor)
            drives.append(drive)
        step_list, b_list, c_list, x_list = ([], [], [], [])
        for index in reversed(range(BLOCK)):
            lam = adjoint + c_blk[:, index, :, None] * y_blk[:, index, None, :]
            c_list.append(jnp.sum(y_blk[:, index, None, :] * history[index + 1], axis=2))
            weighted = lam * history[index] * factors[index]
            lam_b = jnp.sum(lam * b_blk[:, index, :, None], axis=1)
            step_list.append(jnp.sum(weighted * decay_rate[None], axis=1) + x_blk[:, index] * lam_b)
            decay_grad = decay_grad + jnp.sum(weighted * steps[:, index, None, :], axis=0)
            b_list.append(jnp.sum(lam * drives[index][:, None, :], axis=2))
            x_list.append(steps[:, index] * lam_b)
            adjoint = factors[index] * lam
        stacked = tuple(
            (jnp.stack(values[::-1], axis=1) for values in (step_list, b_list, c_list, x_list))
        )
        return ((adjoint, decay_grad), stacked)

    initial = (adjoint_in, jnp.zeros(decay_rate.shape, jnp.float32))
    pieces = (
        starts,
        blocks_of(step_size),
        blocks_of(b_in),
        blocks_of(c_out),
        blocks_of(conv_f),
        blocks_of(scan_grad),
    )
    (unused, decay_grad), outputs = lax.scan(retreat, initial, pieces, reverse=True)
    step_grad, b_grad, c_grad, x_grad = (unblock(value) for value in outputs)
    return (step_grad, b_grad, c_grad, x_grad, decay_grad)


def forward_pass(tokens_mb, lengths_mb, full):
    gain, input_projection, w_conv, b_conv, w_x, w_dt, b_dt, a_log, skip, output_projection = full
    group = tokens_mb.shape[1]
    inner = output_projection.shape[0]
    rank = w_dt.shape[0]
    states = a_log.shape[0]
    positions = lax.axis_index("seq") * group + jnp.arange(group, dtype=jnp.int32)
    valid = (positions[None, :] < lengths_mb[:, None]).astype(jnp.float32)
    inputs = tokens_mb.astype(jnp.float32)
    scale = lax.rsqrt(jnp.mean(inputs * inputs, axis=-1, keepdims=True) + EPSILON)
    normalized_input = (inputs * scale * gain.astype(jnp.float32)).astype(jnp.bfloat16)
    mixer_output = jnp.einsum(
        "cwn,ni->cwi", normalized_input, input_projection, preferred_element_type=jnp.float32
    )
    branch_in = mixer_output[..., :inner].astype(jnp.bfloat16)
    gate_pre = mixer_output[..., inner:]
    previous = shifted(branch_in[:, group - (KCONV - 1) :, :], "seq", 1)
    padded = jnp.concatenate([previous, branch_in], axis=1).astype(jnp.float32)
    conv_w = w_conv.astype(jnp.float32)
    conv_pre = b_conv.astype(jnp.float32)[None, None, :] + sum(
        (conv_w[k] * padded[:, k : k + group] for k in range(KCONV))
    )
    conv_out = jax.nn.silu(conv_pre).astype(jnp.bfloat16)
    conv_f = conv_out.astype(jnp.float32)
    proj = jnp.einsum("slc,cr->slr", conv_out, w_x, preferred_element_type=jnp.float32)
    step_low = proj[..., :rank].astype(jnp.bfloat16)
    b_in = proj[..., rank : rank + states]
    c_out = proj[..., rank + states :]
    step_pre = jnp.einsum(
        "slr,rc->slc", step_low, w_dt, preferred_element_type=jnp.float32
    ) + b_dt.astype(jnp.float32)
    step_size = jax.nn.softplus(step_pre)
    decay_rate = -jnp.exp(a_log.astype(jnp.float32))
    lower = (jnp.arange(group)[:, None] >= jnp.arange(group)[None, :]).astype(jnp.float32)
    running = jnp.einsum(
        "tu,suc->stc",
        lower,
        step_size,
        precision=lax.Precision.HIGHEST,
        preferred_element_type=jnp.float32,
    )
    total = running[:, -1]
    decay_total = jnp.exp(decay_rate[None] * total[:, None, :])
    state_sum = weighted_total(total[:, None, :] - running, b_in, step_size * conv_f, decay_rate)
    unused, state_in = prefix(
        (decay_total, state_sum),
        "seq",
        affine_join,
        (jnp.ones_like(decay_total), jnp.zeros_like(state_sum)),
    )
    outputs, starts = run_forward(state_in, step_size, b_in, c_out, conv_f, decay_rate)
    scan_out = outputs + skip.astype(jnp.float32) * conv_f
    gated_output = (scan_out * jax.nn.silu(gate_pre)).astype(jnp.bfloat16)
    residual_branch = jnp.einsum(
        "ejw,wx->ejx", gated_output, output_projection, preferred_element_type=jnp.float32
    )
    result = (valid[..., None] * (inputs + residual_branch)).astype(jnp.bfloat16)
    saved = (
        valid,
        inputs,
        scale,
        normalized_input,
        gate_pre,
        padded,
        conv_pre,
        conv_out,
        conv_f,
        step_low,
        b_in,
        c_out,
        step_pre,
        step_size,
        running,
        decay_total,
        starts,
        scan_out,
        gated_output,
    )
    return (result, saved)


def backward_pass(saved, cotangent_mb, full):
    gain, input_projection, w_conv, b_conv, w_x, w_dt, b_dt, a_log, skip, output_projection = full
    (
        valid,
        inputs,
        scale,
        normalized_input,
        gate_pre,
        padded,
        conv_pre,
        conv_out,
        conv_f,
        step_low,
        b_in,
        c_out,
        step_pre,
        step_size,
        running,
        decay_total,
        starts,
        scan_out,
        gated_output,
    ) = saved
    group = inputs.shape[1]
    decay_rate = -jnp.exp(a_log.astype(jnp.float32))
    out_grad = valid[..., None] * cotangent_mb.astype(jnp.float32)
    output_lowered = out_grad.astype(jnp.bfloat16)
    output_weight_grad = jnp.einsum(
        "jfw,jfm->wm", gated_output, output_lowered, preferred_element_type=jnp.float32
    )
    gated_output_grad = jnp.einsum(
        "wkx,yx->wky", output_lowered, output_projection, preferred_element_type=jnp.float32
    )
    gate_sig = jax.nn.sigmoid(gate_pre)
    scan_grad = gated_output_grad * gate_pre * gate_sig
    gate_grad = gated_output_grad * scan_out * gate_sig * (1.0 + gate_pre * (1.0 - gate_sig))
    skip_grad = jnp.sum(scan_grad * conv_f, axis=(0, 1))
    adjoint_sum = weighted_total(running, c_out, scan_grad, decay_rate)
    unused, adjoint_in = entering(
        (decay_total, adjoint_sum),
        "seq",
        affine_join,
        (jnp.ones_like(decay_total), jnp.zeros_like(adjoint_sum)),
    )
    step_grad, b_grad, c_grad, x_scan_grad, decay_grad = run_backward(
        adjoint_in, starts, step_size, b_in, c_out, conv_f, scan_grad, decay_rate
    )
    a_log_grad = decay_grad * decay_rate
    pre_grad = step_grad * jax.nn.sigmoid(step_pre)
    bias_dt_grad = jnp.sum(pre_grad, axis=(0, 1))
    pre_low = pre_grad.astype(jnp.bfloat16)
    grad_dt_w = jnp.einsum("slr,slc->rc", step_low, pre_low, preferred_element_type=jnp.float32)
    rank_grad = jnp.einsum("slc,rc->slr", pre_low, w_dt, preferred_element_type=jnp.float32)
    proj_grad = jnp.concatenate([rank_grad, b_grad, c_grad], axis=-1).astype(jnp.bfloat16)
    grad_x_w = jnp.einsum("slc,slr->cr", conv_out, proj_grad, preferred_element_type=jnp.float32)
    conv_grad = (
        jnp.einsum("slr,cr->slc", proj_grad, w_x, preferred_element_type=jnp.float32)
        + x_scan_grad
        + skip.astype(jnp.float32) * scan_grad
    )
    conv_sig = jax.nn.sigmoid(conv_pre)
    pre_conv_grad = conv_grad * conv_sig * (1.0 + conv_pre * (1.0 - conv_sig))
    conv_bias_grad = jnp.sum(pre_conv_grad, axis=(0, 1))
    conv_w_grad = jnp.stack(
        [jnp.sum(pre_conv_grad * padded[:, k : k + group], axis=(0, 1)) for k in range(KCONV)]
    )
    conv_w = w_conv.astype(jnp.float32)
    padded_grad = sum(
        (
            jnp.pad(conv_w[k] * pre_conv_grad, ((0, 0), (k, KCONV - 1 - k), (0, 0)))
            for k in range(KCONV)
        )
    )
    edge_back = shifted(for_sending(padded_grad[:, : KCONV - 1]), "seq", -1)
    branch_grad = padded_grad[:, KCONV - 1 :] + jnp.pad(
        edge_back, ((0, 0), (group - (KCONV - 1), 0), (0, 0))
    )
    mixer_output_grad = jnp.concatenate([branch_grad, gate_grad], axis=-1).astype(jnp.bfloat16)
    input_weight_grad = jnp.einsum(
        "ang,anr->gr", normalized_input, mixer_output_grad, preferred_element_type=jnp.float32
    )
    normalized_input_grad = jnp.einsum(
        "ujg,wg->ujw", mixer_output_grad, input_projection, preferred_element_type=jnp.float32
    )
    gain_grad = jnp.sum(normalized_input_grad * inputs * scale, axis=(0, 1))
    weighted = normalized_input_grad * gain.astype(jnp.float32)
    input_grad = (
        out_grad
        + scale * weighted
        - inputs * scale * scale * scale * jnp.mean(weighted * inputs, axis=-1, keepdims=True)
    )
    grads = (
        gain_grad,
        input_weight_grad,
        conv_w_grad,
        conv_bias_grad,
        grad_x_w,
        grad_dt_w,
        bias_dt_grad,
        a_log_grad,
        skip_grad,
        output_weight_grad,
    )
    return (input_grad.astype(jnp.bfloat16), grads)


def body(
    tokens,
    lengths,
    cotangent,
    norm_gain,
    in_weight,
    conv_weight,
    conv_bias,
    x_weight,
    dt_weight,
    dt_bias,
    a_log,
    skip_d,
    out_weight,
):
    shards = (
        norm_gain,
        in_weight,
        conv_weight,
        conv_bias,
        x_weight,
        dt_weight,
        dt_bias,
        a_log,
        skip_d,
        out_weight,
    )
    results = []
    input_grads = []
    owned = None
    for micro in range(tokens.shape[0]):
        forward_full = gather_forward(shards)
        result, saved = forward_pass(tokens[micro], lengths[micro], forward_full)
        backward_full = gather_backward(shards)
        input_grad, grads = backward_pass(saved, cotangent[micro], backward_full)
        results.append(result)
        input_grads.append(input_grad)
        shares = scatter_each(grads)
        owned = (
            shares
            if owned is None
            else tuple((first + second for first, second in zip(owned, shares)))
        )
    block_out = jnp.stack(results, axis=0)
    grad_input = jnp.stack(input_grads, axis=0)
    return (
        block_out,
        grad_input,
        owned[0],
        owned[1],
        owned[2],
        owned[3],
        owned[4],
        owned[5],
        owned[6],
        owned[7],
        owned[8],
        owned[9],
    )


def solution(mesh):
    placed = (
        P(None, "dp", "seq", None),
        P(None, "dp"),
        P(None, "dp", "seq", None),
        P(("dp", "seq")),
        P(("dp", "seq"), None),
        P(None, ("dp", "seq")),
        P(("dp", "seq")),
        P(("dp", "seq"), None),
        P(None, ("dp", "seq")),
        P(("dp", "seq")),
        P(None, ("dp", "seq")),
        P(("dp", "seq")),
        P(("dp", "seq"), None),
    )
    return jax.shard_map(
        body,
        mesh=mesh,
        in_specs=placed,
        out_specs=(
            P(None, "dp", "seq", None),
            P(None, "dp", "seq", None),
            P(("dp", "seq")),
            P(("dp", "seq"), None),
            P(None, ("dp", "seq")),
            P(("dp", "seq")),
            P(("dp", "seq"), None),
            P(None, ("dp", "seq")),
            P(("dp", "seq")),
            P(None, ("dp", "seq")),
            P(("dp", "seq")),
            P(("dp", "seq"), None),
        ),
        check_vma=False,
    )
```

profile of v0, /device:TPU:0, one launch (start us, length us, event | category | flops | bytes accessed | tf_op | source)
XLA Modules:
  0.0 4398.0 jit_solution(898500987257257387)
XLA Ops:
  11.0 43.4 all-reduce.10
  59.1 42.4 all_gather.106
  101.7 37.6 all-gather.8
  139.3 39.3 all-gather.9
  178.6 39.2 all_gather.104
  217.8 39.3 all-gather.10
  270.8 54.7 %all-gather.20.cloned.1.call-done = bf16[2048,8192]{1,0:T(8,128)(2,1)} async-done(((bf16[64,8192]{1,0:T(8,128)(2,1)}), bf16[2048,8192]{1,0:T(8,128)(2,1)}) %all-gather.20.cloned.1.call-update) | async-done | bytes 33554448 | tf_op jit(solution)/shard_map/all_gather | solution.py:83
  376.0 33.0 multiply_reduce_fusion.133
  459.8 43.8 while.188
  505.8 43.8 while.184
  576.8 126.5 %while.182 = (s32[]{:T(128)}, f32[1,16,4096]{2,1,0:T(8,128)S(1)}, f32[16,1,16,4096]{3,2,1,0:T(8,128)}, f32[16,1,16,4096]{3,2,1,0:T(8,128)}, f32[16,1,16,4096]{3,...) while((s32[]{:T(128)}, f32[1,16,4096]{2,1,0:T(8,128)S(1)}, ...), condition=%wide.region_23.24_spmd, body=%wide.region_6.23_spmd.sunk | while | flops 9437186 | bytes 9252213 | solution.py:160
  704.1 43.8 while.191
  748.7 43.8 while.186
  825.1 127.6 %while.183 = (s32[]{:T(128)}, f32[1,16,4096]{2,1,0:T(8,128)S(1)}, f32[16,1,16,4096]{3,2,1,0:T(8,128)}, f32[16,1,16,4096]{3,2,1,0:T(8,128)}, f32[16,1,16,4096]{3,...) while((s32[]{:T(128)}, f32[1,16,4096]{2,1,0:T(8,128)S(1)}, ...), condition=%wide.region_47.48_spmd, body=%wide.region_30.47_spmd.sunk | while | flops 9437186 | bytes 9252213 | solution.py:160
  964.2 884.4 %while.190 = (s32[]{:T(128)}, f32[1,16,4096]{2,1,0:T(8,128)S(1)}, f32[16,4096]{1,0:T(8,128)}, f32[16,1,16,4096]{3,2,1,0:T(8,128)}, bf16[16,1,16,16]{3,2,1,0:T(8,...) while((s32[]{:T(128)}, f32[1,16,4096]{2,1,0:T(8,128)S(1)}, ...), condition=%wide.region_118.119_spmd.clone, body=%wide.region_53.118_spmd.clone.sunk | while | flops 44498436 | bytes 31232556 | solution.py:209
  1859.9 874.3 %while.193 = (s32[]{:T(128)}, f32[1,16,4096]{2,1,0:T(8,128)S(1)}, f32[16,4096]{1,0:T(8,128)}, f32[16,1,16,4096]{3,2,1,0:T(8,128)}, bf16[16,1,16,16]{3,2,1,0:T(8,...) while((s32[]{:T(128)}, f32[1,16,4096]{2,1,0:T(8,128)S(1)}, ...), condition=%wide.region_190.191_spmd.clone, body=%wide.region_125.190_spmd.clone.sunk | while | flops 44498436 | bytes 31232556 | solution.py:209
  2819.3 24.9 convolution_add_fusion.1
  2866.4 26.0 fusion.187
  2892.3 44.2 %convolution_add_fusion = f32[2048,8192]{1,0:T(8,128)} fusion(f32[2048,8192]{1,0:T(8,128)} %fusion.187, bf16[256,4096]{1,0:T(8,128)(2,1)} %get-tuple-element.2570, bf16[256,4096]{1,0:T(8,128)(2,1)} %fusion.236, f32[256]{0:T(256)S(1)} %copy-done.125, f32[2048]{0:T(1024)S(1)} %copy-done.81, bf16[2,1,256,2048]{3,2,1,0:T(8,128)(2,1)S(1)} %copy-done.9), kind=kOutput, calls=%fused_computation.866 | convolution fusion | flops 8617197568 | bytes 139469824 | tf_op jit(solution)/shard_map/ang,anr->gr/dot_general | solution.py:373
  2992.9 42.3 all-reduce.15
  3055.2 136.7 %reduce-scatter.13.cloned.1.call-done = f32[128,128]{1,0:T(8,128)} async-done(((f32[128,4096]{1,0:T(8,128)}), f32[128,128]{1,0:T(8,128)}) %reduce-scatter.13.cloned.1.call-update) | async-done | bytes 65552 | tf_op jit(solution)/shard_map/reduce_scatter | solution.py:119
  3191.9 137.7 %reduce-scatter.11.cloned.1.call-done = f32[128,160]{0,1:T(8,128)} async-done(((f32[4096,160]{0,1:T(8,128)}), f32[128,160]{0,1:T(8,128)}) %reduce-scatter.11.cloned.1.call-update) | async-done | bytes 81936 | tf_op jit(solution)/shard_map/reduce_scatter | solution.py:118
  3329.6 353.0 %reduce-scatter.17.cloned.1.call-done = f32[128,2048]{1,0:T(8,128)} async-done(((f32[4096,2048]{1,0:T(8,128)}), f32[128,2048]{1,0:T(8,128)}) %reduce-scatter.17.cloned.1.call-update) | async-done | bytes 1048592 | tf_op jit(solution)/shard_map/reduce_scatter | solution.py:123
  3682.6 708.7 %reduce-scatter.9.cloned.1.call-done = f32[64,8192]{1,0:T(8,128)} async-done(((f32[2048,8192]{1,0:T(8,128)}), f32[64,8192]{1,0:T(8,128)}) %reduce-scatter.9.cloned.1.call-update) | async-done | bytes 2097168 | tf_op jit(solution)/shard_map/reduce_scatter | solution.py:115
  (4885 shorter events, 2575.3 us)
Async XLA Ops:
  7.2 250.5 %all-gather.26.cloned.1.call-start = ((), (), s32[]{:S(2)}) async-start(), calls=%async_computation.9 | async-start | bytes 17301504 | tf_op jit(solution)/shard_map/all_gather | solution.py:91
  7.9 317.6 %all-gather.20.cloned.1.call-start = ((), (), s32[]{:S(2)}) async-start(), calls=%async_computation.6 | async-start | bytes 34603008 | tf_op jit(solution)/shard_map/all_gather | solution.py:83
  8.7 400.4 %all-gather.22.cloned.1.call-start = ((), (), s32[]{:S(2)}) async-start(), calls=%async_computation.7 | async-start | bytes 1351680 | tf_op jit(solution)/shard_map/all_gather | solution.py:86
  9.4 417.0 %all-gather.24.cloned.1.call-start = ((), (), s32[]{:S(2)}) async-start(), calls=%async_computation.8 | async-start | bytes 1081344 | tf_op jit(solution)/shard_map/all_gather | solution.py:87
  10.0 942.8 %all-gather.30.cloned.1.call-start = ((), (), s32[]{:S(2)}) async-start(), calls=%async_computation.11 | async-start | bytes 1310720 | tf_op jit(solution)/shard_map/all_gather | solution.py:44
  54.4 292.1 %copy-start.80 = (f32[2048]{0:T(1024)}, f32[2048]{0:T(1024)S(1)}, u32[]{:S(2)}) copy-start(f32[2048]{0:T(1024)S(1)} %convert_element_type.414) | copy-start | bytes 24580
  59.1 316.9 %copy-start.152 = (f32[256]{0:T(256)}, f32[256]{0:T(256)S(1)}, u32[]{:S(2)}) copy-start(f32[256]{0:T(256)S(1)} %compare_convert_fusion.1) | copy-start | bytes 3076
  101.6 274.4 %copy-start.144 = (f32[1,4096]{1,0:T(1,128)}, f32[1,4096]{1,0:T(1,128)S(1)}, u32[]{:S(2)}) copy-start(f32[1,4096]{1,0:T(1,128)S(1)} %get-tuple-element.2599) | copy-start | bytes 49156
  101.6 274.4 %copy-start.146 = (f32[1,4096]{1,0:T(1,128)}, f32[1,4096]{1,0:T(1,128)S(1)}, u32[]{:S(2)}) copy-start(f32[1,4096]{1,0:T(1,128)S(1)} %get-tuple-element.2600) | copy-start | bytes 49156
  101.6 274.4 %copy-start.148 = (f32[1,4096]{1,0:T(1,128)}, f32[1,4096]{1,0:T(1,128)S(1)}, u32[]{:S(2)}) copy-start(f32[1,4096]{1,0:T(1,128)S(1)} %get-tuple-element.2601) | copy-start | bytes 49156
  344.1 26.5 collective-permute-start
  367.5 5.9 collective-permute-start.1
  504.3 448.5 %all-gather.28.cloned.1.call-start = ((), (), s32[]{:S(2)}) async-start(), calls=%async_computation.10 | async-start | bytes 1310720 | tf_op jit(solution)/shard_map/all_gather | solution.py:44
  807.6 1040.9 %all-gather.34.cloned.1.call-start = ((), (), s32[]{:S(2)}) async-start(), calls=%async_computation.13 | async-start | bytes 1310720 | tf_op jit(solution)/shard_map/all_gather | solution.py:44
  820.2 1028.4 %all-gather.32.cloned.1.call-start = ((), (), s32[]{:S(2)}) async-start(), calls=%async_computation.12 | async-start | bytes 1310720 | tf_op jit(solution)/shard_map/all_gather | solution.py:44
  952.7 2090.1 %reduce-scatter.19.cloned.1.call-start = ((), (), s32[]{:S(2)}) async-start(), calls=%async_computation.19 | async-start | bytes 2162688
  964.2 884.4 %copy-start.1 = (f32[1,16,4096]{2,1,0:T(8,128)S(1)}, f32[1,16,4096]{2,1,0:T(8,128)}, u32[]{:S(2)}) copy-start(f32[1,16,4096]{2,1,0:T(8,128)} %custom-call.8) | copy-start | bytes 786436
  2783.4 271.8 %reduce-scatter.15.cloned.1.call-start = ((), (), s32[]{:S(2)}) async-start(), calls=%async_computation.17 | async-start | bytes 270336 | tf_op jit(solution)/shard_map/reduce_scatter | solution.py:121
  2784.2 407.6 %reduce-scatter.13.cloned.1.call-start = ((), (), s32[]{:S(2)}) async-start(), calls=%async_computation.16 | async-start | bytes 2162688 | tf_op jit(solution)/shard_map/reduce_scatter | solution.py:119
  2788.4 541.2 %reduce-scatter.11.cloned.1.call-start = ((), (), s32[]{:S(2)}) async-start(), calls=%async_computation.15 | async-start | bytes 2703360 | tf_op jit(solution)/shard_map/reduce_scatter | solution.py:118
  2792.2 890.4 %reduce-scatter.17.cloned.1.call-start = ((), (), s32[]{:S(2)}) async-start(), calls=%async_computation.18 | async-start | bytes 34603008 | tf_op jit(solution)/shard_map/reduce_scatter | solution.py:123
  2844.2 1547.1 %reduce-scatter.9.cloned.1.call-start = ((), (), s32[]{:S(2)}) async-start(), calls=%async_computation.14 | async-start | bytes 69206016 | tf_op jit(solution)/shard_map/reduce_scatter | solution.py:115
  2852.6 9.6 collective-permute-start.2
  2860.8 3.7 collective-permute-start.3
  (1323 other events, 19435.4 us)
Sparse Core Ops, SparseCore 0:
  10.9 118.4 all-gather.25
  132.3 193.1 all-gather.19
  328.3 47.5 all-gather.21
  378.6 47.7 all-gather.23
  504.4 16.2 all-gather.29
  807.8 16.2 all-gather.27
  825.6 16.6 all-gather.33
  952.8 16.1 all-gather.31
  2783.5 137.4 reduce-scatter.18
  2923.6 131.4 reduce-scatter.14
  3058.0 133.8 reduce-scatter.12
  3194.6 134.9 reduce-scatter.10
  3332.5 350.0 reduce-scatter.16
  3685.4 705.8 reduce-scatter.8
where the time goes:
time: 4470 us; the launch traced here: 4400 us
  other arithmetic  1530 us (34%)
  waiting for transfers between devices  1420 us (32%)
  local copies, waits for them, and re-layouts  782 us (17%)
  blocking collectives  314 us (7%)
  matrix products  308 us (7%)
    reduce_scatter x1, waiting for transfers between devices, scatter_each(): lax.psum_scatter(g_in, ('dp', 'seq'), scatter_dimension=0, tiled=True)  709 us
    reduce_scatter x1, waiting for transfers between devices, scatter_each(): lax.psum_scatter(g_out, ('dp', 'seq'), scatter_dimension=0, tiled=True)  353 us
    reduce_sum x160, other arithmetic, retreat(): b_list.append(jnp.sum(lam * drives[index][:, None, :], axis=2))  349 us
    reduce_sum x160, other arithmetic, retreat(): jnp.sum(weighted * decay_rate[None], axis=1) + x_blk[:, index] * lam_b  272 us
    squeeze x288, local copies, waits for them, and re-layouts, weighted_total(): lax.scan(add_block, initial, (blocks_of(exponent), blocks_of(left), block...  246 us
    reduce_sum x128, other arithmetic, retreat(): jnp.sum(y_blk[:, index, None, :] * history[index + 1], axis=2)  220 us
    another operation x128, local copies, waits for them, and re-layouts, retreat(): jnp.stack(values[::-1], axis=1)  208 us
    add x96, other arithmetic, retreat(): jnp.sum(weighted * decay_rate[None], axis=1) + x_blk[:, index] * lam_b  155 us

commit v1 on v0

v1 whole, which is shorter than its diff:
```python
import jax
import jax.numpy as jnp
from jax import lax
from jax.experimental import pallas as pl
from jax.experimental.pallas import tpu as pltpu
from jax.sharding import PartitionSpec as P

F32 = jnp.float32
BF16 = jnp.bfloat16
LOG2E = 1.4426950408889634
CHUNK = 128
KCONV = 4
EPSILON = 1e-05


def softplus(v):
    return jnp.maximum(v, 0.0) + jnp.log1p(jnp.exp(-jnp.abs(v)))


def expand_states(bc_ref, spread):
    rows, length = bc_ref.shape
    for t in range(length):
        spread[t * rows:(t + 1) * rows, :] = jnp.broadcast_to(bc_ref[:, t:t + 1], (rows, 128))


def lanes_of(value, width):
    return jnp.concatenate([value] * (width // 128), axis=1) if width > 128 else value


def fold(value, width):
    total = value[:, 0:128]
    for at in range(128, width, 128):
        total = total + value[:, at:at + 128]
    return total


def scan_forward_kernel(order, proj_ref, x_ref, dtw_ref, dtb_ref, alog_ref, skip_ref, held_ref,
                        y_ref, start_ref, state, steps, drive, spread, part, ysum, *, width):
    length, inner = x_ref.shape

    @pl.when(pl.program_id(0) == 0)
    def _():
        state[...] = jnp.zeros_like(state)

    start_ref[0] = state[...]
    xs = x_ref[...].astype(F32)
    pre = jnp.dot(proj_ref[0:length, :].astype(BF16), dtw_ref[...], preferred_element_type=F32) + dtb_ref[...]
    step = softplus(pre)
    steps[...] = step
    drive[...] = step * xs
    expand_states(proj_ref.at[length:, :], spread)
    blocks = width // 128

    def group(g, _):
        lanes = pl.ds(pl.multiple_of(g * width, width), width)
        rate = -jnp.exp(alog_ref[:, lanes].astype(F32)) * LOG2E

        def eight(i, h):
            base = pl.multiple_of(i * 8, 8)
            for r in range(8):
                st = steps[pl.ds(base + r, 1), lanes]
                dr = drive[pl.ds(base + r, 1), lanes]
                at = (base + r) * 32
                b = lanes_of(spread[pl.ds(pl.multiple_of(at, 32), 16), :], width)
                c = lanes_of(spread[pl.ds(pl.multiple_of(at + 16, 16), 16), :], width)
                h = jnp.exp2(st * rate) * h + b * dr
                p = c * h
                p = p[0:8] + p[8:16]
                for j in range(blocks):
                    part[j, r * 8:(r + 1) * 8, :] = p[:, j * 128:(j + 1) * 128]
            for j in range(blocks):
                total = part[j, pl.ds(0, 8, stride=8), :]
                for k in range(1, 8):
                    total = total + part[j, pl.ds(k, 8, stride=8), :]
                ysum[pl.ds(base, 8), pl.ds(pl.multiple_of(g * width + j * 128, 128), 128)] = total
            return h

        state[:, lanes] = lax.fori_loop(0, length // 8, eight, state[:, lanes])
        return 0

    lax.fori_loop(0, inner // width, group, 0)
    y_ref[...] = (ysum[...] + skip_ref[...] * xs).astype(y_ref.dtype)


def spec_nat(length, cols):
    return pl.BlockSpec((length, cols), lambda i, order: (i, 0))


def whole_spec(shape):
    return pl.BlockSpec(shape, lambda i, order: (0,) * len(shape))


def placed(per_piece, count, reverse=False, base=0):
    def index(i, order):
        at = count - 1 - i if reverse else i
        return (order[at // per_piece] * per_piece + at % per_piece + base, 0)
    return index


def scan_forward(order, proj, x, dtw, dtb, alog, skip, micro, micros, held, width=512):
    length, inner = x.shape
    count = length // CHUNK
    states = alog.shape[0]
    rank = dtw.shape[0]
    per_piece = count // order.shape[0]
    width = min(width, inner)
    first = held is None
    return pl.pallas_call(
        lambda *refs: scan_forward_kernel(*refs, width=width),
        grid_spec=pltpu.PrefetchScalarGridSpec(
            num_scalar_prefetch=1,
            grid=(count,),
            in_specs=[
                spec_nat(CHUNK + 2 * states, rank), spec_nat(CHUNK, inner),
                whole_spec((rank, inner)), whole_spec((1, inner)), whole_spec((states, inner)), whole_spec((1, inner)),
                pl.BlockSpec(memory_space=pl.ANY),
            ],
            out_specs=[
                pl.BlockSpec((CHUNK, inner), placed(per_piece, count, False, micro * count)),
                pl.BlockSpec((1, states, inner), lambda i, order: (i, 0, 0)),
            ],
            scratch_shapes=[
                pltpu.VMEM((states, inner), F32),
                pltpu.VMEM((CHUNK, inner), F32),
                pltpu.VMEM((CHUNK, inner), F32),
                pltpu.VMEM((CHUNK * 2 * states, 128), F32),
                pltpu.VMEM((width // 128, 64, 128), F32),
                pltpu.VMEM((CHUNK, inner), F32),
            ],
        ),
        out_shape=[
            jax.ShapeDtypeStruct((micros * length, inner), BF16),
            jax.ShapeDtypeStruct((count, states, inner), F32),
        ],
        input_output_aliases={} if first else {7: 0},
        name="scan_forward",
    )(order, proj, x, dtw, dtb, alog, skip, dtb if first else held)


def scan_backward_kernel(order, proj_ref, x_ref, sg_ref, start_ref, dtw_ref, dtb_ref, alog_ref, skip_ref,
                         pg_ref, xg_ref, gdtw_ref, gdtb_ref, galog_ref, gskip_ref,
                         adjoint, steps, drive, grads, spread, hist, fac, bsum, csum, part, part2, lamb, stepg, *, width):
    length, inner = x_ref.shape
    first = pl.program_id(0) == 0

    @pl.when(first)
    def _():
        adjoint[...] = jnp.zeros_like(adjoint)
        gdtw_ref[...] = jnp.zeros_like(gdtw_ref)
        gdtb_ref[...] = jnp.zeros_like(gdtb_ref)
        galog_ref[...] = jnp.zeros_like(galog_ref)
        gskip_ref[...] = jnp.zeros_like(gskip_ref)

    xs = x_ref[...].astype(F32)
    low = proj_ref[0:length, :].astype(BF16)
    pre = jnp.dot(low, dtw_ref[...], preferred_element_type=F32) + dtb_ref[...]
    step = softplus(pre)
    steps[...] = step
    drive[...] = step * xs
    grads[...] = sg_ref[...].astype(F32)
    expand_states(proj_ref.at[length:, :], spread)
    bsum[...] = jnp.zeros_like(bsum)
    csum[...] = jnp.zeros_like(csum)
    blocks = width // 128

    def group(g, _):
        lanes = pl.ds(pl.multiple_of(g * width, width), width)
        decay = -jnp.exp(alog_ref[:, lanes].astype(F32))
        rate = decay * LOG2E

        def again(i, h):
            base = pl.multiple_of(i * 8, 8)
            for r in range(8):
                st = steps[pl.ds(base + r, 1), lanes]
                dr = drive[pl.ds(base + r, 1), lanes]
                sg = grads[pl.ds(base + r, 1), lanes]
                b = lanes_of(spread[pl.ds(pl.multiple_of((base + r) * 32, 32), 16), :], width)
                row = pl.ds(pl.multiple_of((base + r) * 16, 16), 16)
                hist[row, :] = h
                a = jnp.exp2(st * rate)
                fac[row, :] = a
                h = a * h + b * dr
                csum[row, :] += fold(sg * h, width)
            return h

        lax.fori_loop(0, length // 8, again, start_ref[0, :, lanes])

        def back(i, carry):
            adj, dsum = carry
            base = pl.multiple_of(length - 8 - i * 8, 8)
            for r in reversed(range(8)):
                st = steps[pl.ds(base + r, 1), lanes]
                dr = drive[pl.ds(base + r, 1), lanes]
                sg = grads[pl.ds(base + r, 1), lanes]
                at = (base + r) * 32
                b = lanes_of(spread[pl.ds(pl.multiple_of(at, 32), 16), :], width)
                c = lanes_of(spread[pl.ds(pl.multiple_of(at + 16, 16), 16), :], width)
                row = pl.ds(pl.multiple_of((base + r) * 16, 16), 16)
                lam = adj + c * sg
                bsum[row, :] += fold(lam * dr, width)
                adj = fac[row, :] * lam
                w = adj * hist[row, :]
                dsum = dsum + w * st
                p = lam * b
                p = p[0:8] + p[8:16]
                q = w * decay
                q = q[0:8] + q[8:16]
                for j in range(blocks):
                    part[j, r * 8:(r + 1) * 8, :] = p[:, j * 128:(j + 1) * 128]
                    part2[j, r * 8:(r + 1) * 8, :] = q[:, j * 128:(j + 1) * 128]
            for j in range(blocks):
                total = part[j, pl.ds(0, 8, stride=8), :]
                total2 = part2[j, pl.ds(0, 8, stride=8), :]
                for k in range(1, 8):
                    total = total + part[j, pl.ds(k, 8, stride=8), :]
                    total2 = total2 + part2[j, pl.ds(k, 8, stride=8), :]
                where = pl.ds(pl.multiple_of(g * width + j * 128, 128), 128)
                lamb[pl.ds(base, 8), where] = total
                stepg[pl.ds(base, 8), where] = total2
            return adj, dsum

        adj, dsum = lax.fori_loop(0, length // 8, back, (adjoint[:, lanes], jnp.zeros((16, width), F32)))
        adjoint[:, lanes] = adj
        galog_ref[:, lanes] += dsum * decay
        return 0

    lax.fori_loop(0, inner // width, group, 0)
    xs = x_ref[...].astype(F32)
    sg = grads[...]
    lam_b = lamb[...]
    low = proj_ref[0:length, :].astype(BF16)
    pre = jnp.dot(low, dtw_ref[...], preferred_element_type=F32) + dtb_ref[...]
    sig = 1.0 / (1.0 + jnp.exp(-pre))
    pre_grad = (stepg[...] + xs * lam_b) * sig
    gdtb_ref[...] += jnp.sum(pre_grad, axis=0, keepdims=True)
    gskip_ref[...] += jnp.sum(sg * xs, axis=0, keepdims=True)
    xg_ref[...] = (steps[...] * lam_b + skip_ref[...] * sg).astype(xg_ref.dtype)
    pre_low = pre_grad.astype(BF16)
    gdtw_ref[...] += lax.dot_general(low, pre_low, (((0,), (0,)), ((), ())), preferred_element_type=F32)
    pg_ref[0:length, :] = lax.dot_general(pre_low, dtw_ref[...], (((1,), (1,)), ((), ())), preferred_element_type=F32)
    states = adjoint.shape[0]
    rows = length * states
    ones = jnp.ones((128, 128), F32)
    token = lax.broadcasted_iota(jnp.int32, (rows, length), 0) // states
    here = token == lax.broadcasted_iota(jnp.int32, (rows, length), 1)
    state = lax.broadcasted_iota(jnp.int32, (states, rows), 1) % states
    pick = (state == lax.broadcasted_iota(jnp.int32, (states, rows), 0)).astype(F32)
    for at, sums in ((length, bsum), (length + states, csum)):
        total = jnp.dot(sums[...], ones, preferred_element_type=F32)
        pg_ref[at:at + states, :] = jnp.dot(pick, jnp.where(here, total, 0.0), preferred_element_type=F32)


def scan_backward(order, proj, x, sg, starts, dtw, dtb, alog, skip, micro, width=512):
    length, inner = x.shape
    count = length // CHUNK
    states = alog.shape[0]
    rank = dtw.shape[0]
    per_piece = count // order.shape[0]
    width = min(width, inner)
    rev = lambda cols: pl.BlockSpec((CHUNK, cols), lambda i, order: (count - 1 - i, 0))
    return pl.pallas_call(
        lambda *refs: scan_backward_kernel(*refs, width=width),
        grid_spec=pltpu.PrefetchScalarGridSpec(
            num_scalar_prefetch=1,
            grid=(count,),
            in_specs=[
                pl.BlockSpec((CHUNK + 2 * states, rank), lambda i, order: (count - 1 - i, 0)), rev(inner),
                pl.BlockSpec((CHUNK, inner), placed(per_piece, count, True, micro * count)),
                pl.BlockSpec((1, states, inner), lambda i, order: (count - 1 - i, 0, 0)),
                whole_spec((rank, inner)), whole_spec((1, inner)), whole_spec((states, inner)), whole_spec((1, inner)),
            ],
            out_specs=[
                pl.BlockSpec((CHUNK + 2 * states, rank), lambda i, order: (count - 1 - i, 0)),
                rev(inner),
                whole_spec((rank, inner)), whole_spec((1, inner)), whole_spec((states, inner)), whole_spec((1, inner)),
            ],
            scratch_shapes=[
                pltpu.VMEM((states, inner), F32),
                pltpu.VMEM((CHUNK, inner), F32),
                pltpu.VMEM((CHUNK, inner), F32),
                pltpu.VMEM((CHUNK, inner), F32),
                pltpu.VMEM((CHUNK * 2 * states, 128), F32),
                pltpu.VMEM((CHUNK * states, width), F32),
                pltpu.VMEM((CHUNK * states, width), F32),
                pltpu.VMEM((CHUNK * states, 128), F32),
                pltpu.VMEM((CHUNK * states, 128), F32),
                pltpu.VMEM((width // 128, 64, 128), F32),
                pltpu.VMEM((width // 128, 64, 128), F32),
                pltpu.VMEM((CHUNK, inner), F32),
                pltpu.VMEM((CHUNK, inner), F32),
            ],
        ),
        out_shape=[
            jax.ShapeDtypeStruct((count * (CHUNK + 2 * states), rank), F32),
            jax.ShapeDtypeStruct((length, inner), BF16),
            jax.ShapeDtypeStruct((rank, inner), F32),
            jax.ShapeDtypeStruct((1, inner), F32),
            jax.ShapeDtypeStruct((states, inner), F32),
            jax.ShapeDtypeStruct((1, inner), F32),
        ],
        name="scan_backward",
    )(order, proj, x, sg, starts, dtw, dtb, alog, skip)


def conv_forward_kernel(order, *refs, peers):
    pieces = refs[:peers]
    gain_ref, wb_ref, cw_ref, cb_ref, xw_ref, held_ref, normed_ref, branch_ref, x_ref, proj_ref, pad = refs[peers:]
    length, inner = x_ref.shape
    at = pl.program_id(0)

    @pl.when(at == 0)
    def _():
        pad[0:8, :] = jnp.zeros((8, inner), F32)

    for p in range(peers):
        @pl.when(order[at] == p)
        def _():
            tokens = pieces[p][...].astype(F32)
            scale = lax.rsqrt(jnp.mean(tokens * tokens, axis=-1, keepdims=True) + EPSILON)
            normed_ref[...] = (tokens * scale * gain_ref[...]).astype(BF16)

    groups = wb_ref.shape[0]
    deep = normed_ref.shape[1] // groups
    branch = sum(jnp.dot(normed_ref[:, d * deep:(d + 1) * deep], wb_ref[d, 0:deep, :], preferred_element_type=F32)
                 for d in range(groups)).astype(BF16)
    branch_ref[...] = branch
    pad[8:8 + length, :] = branch.astype(F32)
    pre = cb_ref[...] + sum(cw_ref[k:k + 1, :] * pad[5 + k:5 + k + length, :] for k in range(KCONV))
    x = (pre / (1.0 + jnp.exp(-pre))).astype(BF16)
    x_ref[...] = x
    rank = proj_ref.shape[1]
    low = lax.dot_general(x, xw_ref[0:rank, :], (((1,), (1,)), ((), ())), preferred_element_type=F32)
    maps = lax.dot_general(xw_ref[rank:, :], x, (((1,), (1,)), ((), ())), preferred_element_type=F32)
    rows = CHUNK + maps.shape[0]
    for at in range(length // CHUNK):
        proj_ref[at * rows:at * rows + CHUNK, :] = low[at * CHUNK:(at + 1) * CHUNK, :]
        proj_ref[at * rows + CHUNK:(at + 1) * rows, :] = maps[:, at * CHUNK:(at + 1) * CHUNK]
    pad[0:8, :] = pad[length:length + 8, :]


def conv_forward(order, pieces, gain, wb, cw, cb, xw, rank, micro, micros, held):
    peers = len(pieces)
    tokens, width = pieces[0].shape
    inner = wb.shape[2]
    cols = xw.shape[0]
    rows = tokens // CHUNK * (CHUNK + cols - rank)
    first = held is None
    return pl.pallas_call(
        lambda *refs: conv_forward_kernel(*refs, peers=peers),
        grid_spec=pltpu.PrefetchScalarGridSpec(
            num_scalar_prefetch=1,
            grid=(peers,),
            in_specs=[whole_spec((tokens, width))] * peers + [
                whole_spec((1, width)),
                whole_spec(wb.shape), whole_spec((KCONV, inner)), whole_spec((1, inner)), whole_spec((cols, inner)),
                pl.BlockSpec(memory_space=pl.ANY),
            ],
            out_specs=[
                pl.BlockSpec((tokens, width), placed(1, peers, False, micro * peers)),
                spec_nat(tokens, inner), spec_nat(tokens, inner), spec_nat(rows, rank),
            ],
            scratch_shapes=[pltpu.VMEM((tokens + 8, inner), F32)],
        ),
        out_shape=[
            jax.ShapeDtypeStruct((micros * peers * tokens, width), BF16),
            jax.ShapeDtypeStruct((peers * tokens, inner), BF16),
            jax.ShapeDtypeStruct((peers * tokens, inner), BF16),
            jax.ShapeDtypeStruct((peers * rows, rank), F32),
        ],
        input_output_aliases={} if first else {peers + 6: 0},
        name="conv_forward",
    )(order, *pieces, gain, wb, cw, cb, xw, gain if first else held)


def conv_backward_kernel(order, pg_ref, xg_ref, branch_ref, prev_ref, x_ref, cw_ref, cb_ref, xw_ref, held_ref,
                         mixed_ref, gxw_ref, gcb_ref, gcw_ref, pad, ahead):
    length, inner = x_ref.shape

    @pl.when(pl.program_id(0) == 0)
    def _():
        ahead[length:length + 8, :] = jnp.zeros((8, inner), F32)
        gxw_ref[...] = jnp.zeros_like(gxw_ref)
        gcb_ref[...] = jnp.zeros_like(gcb_ref)
        gcw_ref[...] = jnp.zeros_like(gcw_ref)

    earliest = pl.program_id(0) == pl.num_programs(0) - 1
    pad[0:8, :] = jnp.where(earliest, 0.0, prev_ref[...].astype(F32)[8:16, :])
    pad[8:8 + length, :] = branch_ref[...].astype(F32)
    pre = cb_ref[...] + sum(cw_ref[k:k + 1, :] * pad[5 + k:5 + k + length, :] for k in range(KCONV))
    sig = 1.0 / (1.0 + jnp.exp(-pre))
    rank = pg_ref.shape[1]
    rows = CHUNK + xw_ref.shape[0] - rank
    low, maps = [], []
    for at in range(length // CHUNK):
        low.append(pg_ref[at * rows:at * rows + CHUNK, :].astype(BF16))
        maps.append(pg_ref[at * rows + CHUNK:(at + 1) * rows, :].astype(BF16))
    low, maps = jnp.concatenate(low, axis=0), jnp.concatenate(maps, axis=1)
    grad = (jnp.dot(low, xw_ref[0:rank, :], preferred_element_type=F32)
            + lax.dot_general(maps, xw_ref[rank:, :], (((0,), (0,)), ((), ())), preferred_element_type=F32)
            + xg_ref[...].astype(F32))
    grad = grad * (sig * (1.0 + pre * (1.0 - sig)))
    ahead[0:length, :] = grad
    gcb_ref[...] += jnp.sum(grad, axis=0, keepdims=True)
    for k in range(KCONV):
        gcw_ref[k:k + 1, :] += jnp.sum(grad * pad[5 + k:5 + k + length, :], axis=0, keepdims=True)
    mixed = sum(cw_ref[k:k + 1, :] * ahead[3 - k:3 - k + length, :] for k in range(KCONV))
    mixed_ref[...] = mixed.astype(BF16)
    gxw_ref[0:rank, :] += lax.dot_general(low, x_ref[...], (((0,), (0,)), ((), ())), preferred_element_type=F32)
    gxw_ref[rank:, :] += jnp.dot(maps, x_ref[...], preferred_element_type=F32)
    ahead[length:length + 8, :] = ahead[0:8, :]


def conv_backward(order, pg, xg, branch, x, cw, cb, xw, micro, micros, held):
    length, inner = x.shape
    tokens = length // order.shape[0]
    count = length // tokens
    cols = xw.shape[0]
    first = held is None
    rank = pg.shape[1]
    rows = pg.shape[0] // count
    rev = lambda width: pl.BlockSpec((tokens, width), lambda i, order: (count - 1 - i, 0))
    return pl.pallas_call(
        conv_backward_kernel,
        grid_spec=pltpu.PrefetchScalarGridSpec(
            num_scalar_prefetch=1,
            grid=(count,),
            in_specs=[
                pl.BlockSpec((rows, rank), lambda i, order: (count - 1 - i, 0)), rev(inner), rev(inner),
                pl.BlockSpec((16, inner), lambda i, order: (jnp.maximum((count - 1 - i) * (tokens // 16) - 1, 0), 0)),
                rev(inner),
                whole_spec((KCONV, inner)), whole_spec((1, inner)), whole_spec((cols, inner)),
                pl.BlockSpec(memory_space=pl.ANY),
            ],
            out_specs=[
                pl.BlockSpec((tokens, inner), placed(1, count, True, micro * count)),
                whole_spec((cols, inner)), whole_spec((1, inner)), whole_spec((KCONV, inner)),
            ],
            scratch_shapes=[pltpu.VMEM((tokens + 8, inner), F32), pltpu.VMEM((tokens + 8, inner), F32)],
        ),
        out_shape=[
            jax.ShapeDtypeStruct((micros * length, inner), BF16),
            jax.ShapeDtypeStruct((cols, inner), F32),
            jax.ShapeDtypeStruct((1, inner), F32),
            jax.ShapeDtypeStruct((KCONV, inner), F32),
        ],
        input_output_aliases={} if first else {9: 0},
        name="conv_backward",
    )(order, pg, xg, branch, branch, x, cw, cb, xw, cb if first else held)


def partner(value, step):
    peers = lax.axis_size("seq")
    return lax.ppermute(value, "seq", [(i, i ^ step) for i in range(peers)])


def halvings():
    step = lax.axis_size("seq") // 2
    while step >= 1:
        yield step
        step //= 2


def reversed_bits(value, peers):
    out = value * 0
    step = 1
    while step < peers:
        out = out * 2 + (value // step) % 2
        step *= 2
    return out


def sum_to_piece(partial, axis):
    for step in reversed(list(halvings())):
        kept, given = jnp.split(partial, 2, axis=axis)
        partial = kept.astype(F32) + partner(given, step).astype(F32)
        if step < lax.axis_size("seq") // 2:
            partial = partial.astype(BF16)
    return partial


def sum_over_pieces(value):
    for step in reversed(list(halvings())[:-1]):
        value = value.astype(F32) + partner(value, step).astype(F32)
        value = value if step == lax.axis_size("seq") // 2 else value.astype(BF16)
    return value


def sum_to_owner(whole):
    ranks = lax.axis_size("dp")
    me = lax.axis_index("dp")
    share = whole.shape[1] // ranks
    parts = jnp.stack([lax.dynamic_slice_in_dim(whole, (me ^ r) * share, share, 1) for r in range(ranks)]).astype(F32)
    step = 1
    while parts.shape[0] > 1:
        parts = parts.reshape((parts.shape[0] // 2, 2) + parts.shape[1:])
        given = parts[:, 1].astype(BF16)
        other = lax.ppermute(given, "dp", [(i, i ^ step) for i in range(ranks)])
        parts = parts[:, 0] + other.astype(F32)
        step *= 2
    return parts[0]


def dot(left, right, dims, kind=F32):
    return lax.dot_general(left, right, (dims, ((), ())), preferred_element_type=kind)


def body(tokens, lengths, cotangent, norm_gain, in_weight, conv_weight, conv_bias, x_weight, dt_weight,
         dt_bias, a_log, skip_d, out_weight):
    micros, slots, piece, width = tokens.shape
    peers, groups = lax.axis_size("seq"), lax.axis_size("dp")
    me = lax.axis_index("seq")
    share = conv_bias.shape[0]
    inner = share * groups
    rows = in_weight.shape[0]
    rank = dt_weight.shape[0]
    states = a_log.shape[0]
    cols = x_weight.shape[1]
    length = piece * peers
    order = reversed_bits(jnp.arange(peers, dtype=jnp.int32) ^ me, peers)
    tokens, cotangent = tokens[:, 0], cotangent[:, 0]

    gain_part = norm_gain
    for step in halvings():
        gain_part = jnp.concatenate([gain_part, partner(gain_part, step)])
    gain_part = gain_part.reshape(peers, rows)
    gain_part = jnp.concatenate([lax.dynamic_slice_in_dim(gain_part, order[q], 1) for q in range(peers)])
    gain_rows = peers * rows // share
    small = jnp.concatenate([
        a_log, conv_weight, conv_bias[None], dt_bias[None], skip_d[None], gain_part.reshape(gain_rows, share),
        jnp.zeros((states - KCONV - 3 - gain_rows, share), BF16), dt_weight, x_weight.T], axis=0)
    packed = small.shape[0]

    def mine(half):
        own = half.reshape(rows, groups, peers, share).transpose(2, 0, 1, 3).reshape(peers * rows, inner)
        return lax.all_to_all(own, "seq", split_axis=0, concat_axis=0, tiled=True)

    first = jnp.concatenate([mine(in_weight[:, :inner * peers]), small.reshape(-1, inner)], axis=0)
    first = lax.all_gather(first, "dp", axis=0, tiled=False)
    pieces = [[tokens[m]] for m in range(micros)]
    for step in halvings():
        for m in range(micros):
            pieces[m] = pieces[m] + [partner(part, step) for part in pieces[m]]
    late, pieces = lax.optimization_barrier((in_weight[:, inner * peers:], pieces))
    wg = lax.all_gather(mine(late), "dp", axis=0, tiled=True)
    wo = lax.all_gather(out_weight, "dp", axis=0, tiled=True)
    small = first[:, peers * rows:].reshape(groups, packed, share)
    at = states + KCONV + 3
    gain = small[:, at:at + gain_rows].reshape(1, width).astype(F32)
    small = jnp.concatenate([small[d] for d in range(groups)], axis=1)
    alog = small[0:states]
    at = states
    cw = small[at:at + KCONV].astype(F32)
    cb = small[at + KCONV:at + KCONV + 1].astype(F32)
    dtb = small[at + KCONV + 1:at + KCONV + 2].astype(F32)
    skip = small[at + KCONV + 2:at + KCONV + 3].astype(F32)
    dtw = small[2 * states:2 * states + rank]
    xw = small[2 * states + rank:]

    convs, normed = [], None
    for m in range(micros):
        normed, branch, x, proj = conv_forward(order, pieces[m], gain, first, cw, cb, xw, rank, m, micros, normed)
        proj = (proj + partner(proj, 1)).astype(BF16)
        if m + 1 < micros:
            proj, pieces[m + 1] = lax.optimization_barrier((proj, pieces[m + 1]))
        convs.append((branch, x, sum_over_pieces(proj)))
    positions = me * piece + jnp.arange(piece, dtype=jnp.int32)
    valid = (positions[None, :] < lengths).astype(F32)[..., None]
    own_grad = (valid * cotangent.astype(F32)).astype(BF16)
    y, starts = None, []
    for m in range(micros):
        y, start = scan_forward(order, convs[m][2], convs[m][1], dtw, dtb, alog, skip, m, micros, y)
        starts.append(start)
        if m == 0:
            grads, y, convs = lax.optimization_barrier(([own_grad], y, convs))
            for step in list(halvings())[:-1]:
                grads = grads + [partner(part, step) for part in grads]
    gate = dot(normed, wg, ((1,), (0,)))
    grads, y = lax.optimization_barrier((grads, y))
    grads = grads + [partner(part, 1) for part in grads]
    out_grad = jnp.concatenate(grads, axis=1).reshape(micros * length, width)
    gg = dot(out_grad, wo, ((1,), (1,)))
    sig = jax.nn.sigmoid(gate)
    yf = y.astype(F32)
    gated = (yf * gate * sig).astype(BF16)
    sg = (gg * gate * sig).astype(BF16)
    gate_grad = (gg * yf * sig * (1.0 + gate * (1.0 - sig))).astype(BF16)
    partial = dot(gated, wo, ((1,), (0,)), BF16).reshape(micros, length, width)
    gwo = dot(gated, out_grad, ((0,), (0,)), BF16)
    gwg = dot(normed, gate_grad, ((0,), (0,)), BF16)
    gwo, gwg, sg, partial = lax.optimization_barrier((gwo, gwg, sg, partial))
    gwo = lax.psum_scatter(gwo, "dp", scatter_dimension=0, tiled=True)
    gwg = lax.psum_scatter(gwg, "dp", scatter_dimension=0, tiled=True)
    gwg = lax.all_to_all(gwg, "seq", split_axis=0, concat_axis=0, tiled=True)
    added = sum_to_piece(partial, 1)
    backs = []
    for m in range(micros):
        given = sg
        if m == micros - 1:
            given, gwo, added = lax.optimization_barrier((given, gwo, added))
            result = (valid * (tokens.astype(F32) + added)).astype(BF16)
        backs.append(list(scan_backward(order, convs[m][2], convs[m][1], given, starts[m], dtw, dtb, alog, skip, m)))
        pg = (backs[m][0] + partner(backs[m][0], 1)).astype(BF16)
        backs[m][0] = sum_over_pieces(pg)
    for m in range(micros - 1):
        backs[m][0], backs[-1][1] = lax.optimization_barrier((backs[m][0], backs[-1][1]))
    w = dot(gate_grad, wg, ((1,), (1,)))
    w, backs[0][0] = lax.optimization_barrier((w, backs[0][0]))
    mixed, totals = None, None
    for m in range(micros):
        pg, xg, gdtw, gdtb, galog, gskip = backs[m]
        if m == micros - 1:
            pg, gwg = lax.optimization_barrier((pg, gwg))
        mixed, gxw, gcb, gcw = conv_backward(order, pg, xg, convs[m][0], convs[m][1], cw, cb, xw, m, micros, mixed)
        part = [galog, gcw, gcb, gdtb, gskip, gdtw, gxw]
        totals = part if totals is None else [a + b for a, b in zip(totals, part)]
    gwb = dot(normed, mixed, ((0,), (0,)), BF16)
    gwb, totals, mixed = lax.optimization_barrier((gwb, totals, mixed))
    gwb = lax.psum_scatter(gwb, "dp", scatter_dimension=0, tiled=True)
    gsmall = sum_to_owner(jnp.concatenate(totals, axis=0))
    wb = first[:, :peers * rows].reshape(width, inner)
    w = w + dot(mixed, wb, ((1,), (1,)))
    w = sum_to_piece(w.astype(BF16).reshape(micros, length, width), 1)
    w, gwb, gsmall = lax.optimization_barrier((w, gwb, gsmall))
    w = w * gain
    inputs = tokens.astype(F32)
    scale = lax.rsqrt(jnp.mean(inputs * inputs, axis=-1, keepdims=True) + EPSILON)
    input_grad = (own_grad.astype(F32) + scale * w - inputs * (scale * scale * scale)
                  * jnp.mean(w * inputs, axis=-1, keepdims=True)).astype(BF16)
    gwb = lax.all_to_all(gwb, "seq", split_axis=0, concat_axis=0, tiled=True)
    spread = lambda g: g.astype(F32).reshape(peers, rows, groups, share).transpose(1, 2, 0, 3).reshape(rows, inner * peers)
    total = jnp.concatenate([spread(gwb), spread(gwg)], axis=1)
    g_gain = jnp.sum(in_weight.astype(F32) * total, axis=1) / norm_gain.astype(F32)
    pieces, at = [], 0
    for count in (states, KCONV, 1, 1, 1, rank, cols):
        pieces.append(gsmall[at:at + count])
        at += count
    galog, gcw, gcb, gdtb, gskip, gdtw, gxw = pieces
    return (
        result[:, None], input_grad[:, None], g_gain, total, gcw, gcb[0], gxw.T, gdtw, gdtb[0], galog, gskip[0],
        gwo.astype(F32),
    )


def solution(mesh):
    placed = (
        P(None, "dp", "seq", None),
        P(None, "dp"),
        P(None, "dp", "seq", None),
        P(("dp", "seq")),
        P(("dp", "seq"), None),
        P(None, ("dp", "seq")),
        P(("dp", "seq")),
        P(("dp", "seq"), None),
        P(None, ("dp", "seq")),
        P(("dp", "seq")),
        P(None, ("dp", "seq")),
        P(("dp", "seq")),
        P(("dp", "seq"), None),
    )
    return jax.shard_map(
        body,
        mesh=mesh,
        in_specs=placed,
        out_specs=(
            P(None, "dp", "seq", None),
            P(None, "dp", "seq", None),
            P(("dp", "seq")),
            P(("dp", "seq"), None),
            P(None, ("dp", "seq")),
            P(("dp", "seq")),
            P(("dp", "seq"), None),
            P(None, ("dp", "seq")),
            P(("dp", "seq")),
            P(None, ("dp", "seq")),
            P(("dp", "seq")),
            P(("dp", "seq"), None),
        ),
        check_vma=False,
    )
```

time: 4470 us -> 732 us (0.16); the launches traced: 4400 us -> 725 us
  other arithmetic: 1530 us -> 51.2 us
  waiting for transfers between devices: 1420 us -> 152 us
  local copies, waits for them, and re-layouts: 782 us -> 38.3 us
  blocking collectives: 314 us -> 11.9 us
  Pallas kernels: 0 us -> 294 us
  matrix products: 308 us -> 122 us
    reduce_scatter x5 -> x3, waiting for transfers between devices: 1350 us -> 3.15 us  [the longest x1 3.14 us: body(): gwb = lax.psum_scatter(gwb, 'dp', scatter_dimension=0, tiled=True)]
    reduce_sum x675 -> x2, other arithmetic: 994 us -> 6 us  [the longest x1 3.27 us: body(): jnp.mean(inputs * inputs, axis=-1, keepdims=True) + EPSILON]
    add x232 -> x16, other arithmetic: 345 us -> 14.1 us  [the longest x2 10.2 us: sum_to_piece(): partial = kept.astype(F32) + partner(given, step).astype(F32)]
    pallas_call x0 -> x8, Pallas kernels: none -> 294 us  [the longest x2 163 us: scan_backward(): pl.pallas_call(lambda *refs: scan_backward_kernel(*refs, width=width), gr...]
    squeeze x288 -> x10, local copies, waits for them, and re-layouts: 246 us -> 1.02 us  [the longest x1 0.52 us: body(): gskip[0]]
    another operation x172 -> x1, local copies, waits for them, and re-layouts: 242 us -> 0.03 us  [sum_to_owner(): jnp.stack([lax.dynamic_slice_in_dim(whole, (me ^ r) * share, share, 1) fo...]
    all_gather x9 -> x0, blocking collectives: 228 us -> none  [the longest x1 42.4 us: gather_forward(): lax.all_gather(w_conv, ('dp', 'seq'), axis=1, tiled=True)]
    dot_general x26 -> x8, matrix products: 308 us -> 122 us  [dot(): lax.dot_general(left, right, (dims, ((), ())), preferred_element_type=kind)]
where the time goes in v1:
time: 732 us; the launch traced here: 725 us
  Pallas kernels  294 us (40%)
  waiting for transfers between devices  152 us (21%)
  matrix products  122 us (17%)
  other arithmetic  51.2 us (7%)
  local copies, waits for them, and re-layouts  38.3 us (5%)
  starting transfers between devices  32.5 us (4%)
  between operations  23.6 us (3%)
  blocking collectives  11.9 us (2%)
    pallas_call x2, Pallas kernels, scan_backward(): pl.pallas_call(lambda *refs: scan_backward_kernel(*refs, width=width), gr...  163 us
    dot_general x8, matrix products, dot(): lax.dot_general(left, right, (dims, ((), ())), preferred_element_type=kind)  122 us
    ppermute x23, waiting for transfers between devices, partner(): return lax.ppermute(value, 'seq', [(i, i ^ step) for i in range(peers)])  112 us
    pallas_call x2, Pallas kernels, scan_forward(): pl.pallas_call(lambda *refs: scan_forward_kernel(*refs, width=width), gri...  66.1 us
    pallas_call x2, Pallas kernels, conv_forward(): pl.pallas_call(lambda *refs: conv_forward_kernel(*refs, peers=peers), gri...  32.9 us
    pallas_call x2, Pallas kernels, conv_backward(): pl.pallas_call(conv_backward_kernel, grid_spec=pltpu.PrefetchScalarGridSp...  31.6 us
    ppermute x3, waiting for transfers between devices, sum_to_owner(): other = lax.ppermute(given, 'dp', [(i, i ^ step) for i in range(ranks)])  19.2 us
    ppermute x23, starting transfers between devices, partner(): return lax.ppermute(value, 'seq', [(i, i ^ step) for i in range(peers)])  17 us
  transfers between devices with their start and end apart: 35, of which 15 were waited for; matrix products, arithmetic and copies ran while one was open for 16% of the time, Pallas kernels for 38%

profile of v1, /device:TPU:0, one launch (start us, length us, event | category | flops | bytes accessed | tf_op | source)
XLA Modules:
  0.0 725.3 jit_solution(7616139032992823062)
XLA Ops:
  30.7 23.5 %collective-permute-done.3.refs_2_ = bf16[256,2048]{1,0:T(8,128)(2,1)S(1)} collective-permute-done((bf16[256,2048]{1,0:T(8,128)(2,1)S(1)}, bf16[256,2048]{1,0:T(8,128)(2,1)S(1)}, u32[]{:S(2)}, u32[]{:S(2)}) %collective-permute-start.3) | collective-permute-done | bytes 1048608 | tf_op jit(solution)/shard_map/ppermute | solution.py:453
  54.2 21.8 %collective-permute-done.refs_2_ = bf16[256,2048]{1,0:T(8,128)(2,1)S(1)} collective-permute-done((bf16[256,2048]{1,0:T(8,128)(2,1)S(1)}, bf16[256,2048]{1,0:T(8,128)(2,1)S(1)}, u32[]{:S(2)}, u32[]{:S(2)}) %collective-permute-start) | collective-permute-done | bytes 1048608 | tf_op jit(solution)/shard_map/ppermute | solution.py:453
  81.4 11.9 %all_to_all.45 = bf16[4,64,1024]{2,1,0:T(8,128)(2,1)} all-to-all(bf16[4,64,1024]{2,1,0:T(8,128)(2,1)S(1)} %all_to_all.33), channel_id=1, replica_groups=mesh['dp'=8,'seq'=4] {'seq'}, dimensions={0} | all-to-all | bytes 1048576 | tf_op jit(solution)/shard_map/all_to_all | solution.py:535
  93.4 17.0 %all-gather.9.cloned.1.call-done = bf16[2368,1024]{1,0:T(8,128)(2,1)} async-done(((bf16[296,1024]{1,0:T(8,128)(2,1)}), bf16[2368,1024]{1,0:T(8,128)(2,1)}) %all-gather.9.cloned.1.call-update) | async-done | bytes 4849680 | tf_op jit(solution)/shard_map/all_gather | solution.py:538
  117.7 16.4 %conv_forward.2 = (bf16[2048,2048]{1,0:T(8,128)(2,1)}, bf16[1024,1024]{1,0:T(8,128)(2,1)}, bf16[1024,1024]{1,0:T(8,128)(2,1)}, f32[1280,128]{1,0:T(8,128)}) custom-call(s32[4]{0:T(128)} %copy-done.29, bf16[256,2048]{1,0:T(8,128)(2,1)} %copy-done.11, bf16[256,2048]{1,0:T(8,128)(2,1)} %copy-done.17, bf16[256,2048]{1,0:T(8,128)(2,1)} %copy-done.18, ...), custom_call_target="tpu_custom_call" | custom-call | tf_op jit(solution)/shard_map/conv_forward/pallas_call | solution.py:348
  137.6 16.5 %conv_forward.3 = (bf16[2048,2048]{1,0:T(8,128)(2,1)}, bf16[1024,1024]{1,0:T(8,128)(2,1)}, bf16[1024,1024]{1,0:T(8,128)(2,1)}, f32[1280,128]{1,0:T(8,128)}) custom-call(s32[4]{0:T(128)} %copy-done.29, bf16[256,2048]{1,0:T(8,128)(2,1)} %copy-done.10, bf16[256,2048]{1,0:T(8,128)(2,1)} %copy-done.14, ...), custom_call_target="tpu_custom_call", output_to_operand_aliasing={{0}: (10, {})} | custom-call | tf_op jit(solution)/shard_map/conv_forward/pallas_call | solution.py:348
  169.0 33.1 %scan_forward.2 = (bf16[2048,1024]{1,0:T(8,128)(2,1)}, f32[8,16,1024]{2,1,0:T(8,128)}) custom-call(s32[4]{0:T(128)} %copy-done.29, f32[1280,128]{1,0:T(8,128)} %convert_add_fusion.6.refs_1_, bf16[1024,1024]{1,0:T(8,128)(2,1)} %get-tuple-element.130.refs_2_.x_ref, bf16[128,1024]{1,0:T(8,128)(2,1)} %slice.190.refs_3_.refs_5_, ...), custom_call_target="tpu_custom_call" | custom-call | tf_op jit(solution)/shard_map/scan_forward/pallas_call | solution.py:108
  204.5 33.0 %scan_forward.3 = (bf16[2048,1024]{1,0:T(8,128)(2,1)}, f32[8,16,1024]{2,1,0:T(8,128)}) custom-call(s32[4]{0:T(128)} %copy-done.29, f32[1280,128]{1,0:T(8,128)} %convert_add_fusion.5.refs_1_, bf16[1024,1024]{1,0:T(8,128)(2,1)} %get-tuple-element.117.refs_2_.x_ref, bf16[128,1024]{1,0:T(8,128)(2,1)} %slice.190.refs_3_.refs_5_, ...), custom_call_target="tpu_custom_call", output_to_operand_aliasing={{0}: (7, {})} | custom-call | tf_op jit(solution)/shard_map/scan_forward/pallas_call | solution.py:108
  237.6 12.1 %collective-permute-done.12 = bf16[2,256,2048]{2,1,0:T(8,128)(2,1)} collective-permute-done((bf16[2,256,2048]{2,1,0:T(8,128)(2,1)S(1)}, bf16[2,256,2048]{2,1,0:T(8,128)(2,1)}, u32[]{:S(2)}, u32[]{:S(2)}) %collective-permute-start.12) | collective-permute-done | bytes 2097184 | tf_op jit(solution)/shard_map/ppermute | solution.py:453
  250.1 14.4 %fusion.29 = f32[2048,1024]{1,0:T(8,128)} fusion(bf16[2048,2048]{1,0:T(8,128)(2,1)} %get-tuple-element.121, bf16[2048,1024]{1,0:T(8,128)(2,1)} %all-gather.5.cloned.1.call-done), kind=kOutput, calls=%fused_computation.113 | convolution fusion | flops 8589934592 | bytes 20971520 | tf_op jit(solution)/shard_map/dot_general | solution.py:504
  271.1 22.3 %multiply_convert_fusion = (bf16[2048,1024]{1,0:T(8,128)(2,1)}, bf16[2048,1024]{1,0:T(8,128)(2,1)}, bf16[2048,1024]{1,0:T(8,128)(2,1)S(1)}) fusion(f32[2048,1024]{1,0:T(8,128)} %fusion.29, bf16[2048,1024]{1,0:T(8,128)(2,1)} %get-tuple-element.120, bf16[2048,2048]{1,0:T(8,128)(2,1)} %bitcast.151, bf16[1024,2048]{1,0:T(8,128)(2,1)} %all-gather.7.cloned.1.call-done), kind=kOutput, calls=%fused_computation.11 | convolution fusion | flops 8625586176 | bytes 37748736 | tf_op jit(solution)/shard_map/dot_general | solution.py:504
  295.5 13.0 %fusion.30 = bf16[1024,2048]{1,0:T(8,128)(2,1)} fusion(bf16[2048,1024]{1,0:T(8,128)(2,1)S(1)} %get-tuple-element.182, bf16[2048,2048]{1,0:T(8,128)(2,1)} %bitcast.152), kind=kOutput, calls=%fused_computation.114 | convolution fusion | flops 8589934592 | bytes 16777216 | tf_op jit(solution)/shard_map/dot_general | solution.py:504
  308.5 14.3 %fusion.31 = bf16[2048,1024]{1,0:T(8,128)(2,1)} fusion(bf16[2048,2048]{1,0:T(8,128)(2,1)} %get-tuple-element.121, bf16[2048,1024]{1,0:T(8,128)(2,1)} %get-tuple-element.181), kind=kOutput, calls=%fused_computation.115 | convolution fusion | flops 8589934592 | bytes 16777216 | tf_op jit(solution)/shard_map/dot_general | solution.py:504
  322.8 14.0 %fusion.32 = bf16[2048,2048]{1,0:T(8,128)(2,1)} fusion(bf16[2048,1024]{1,0:T(8,128)(2,1)} %copy-done.52, bf16[1024,2048]{1,0:T(8,128)(2,1)} %all-gather.7.cloned.1.call-done), kind=kOutput, calls=%fused_computation.116 | convolution fusion | flops 8589934592 | bytes 16777216 | tf_op jit(solution)/shard_map/dot_general | solution.py:504
  359.2 81.8 %scan_backward.2 = (f32[1280,128]{1,0:T(8,128)}, bf16[1024,1024]{1,0:T(8,128)(2,1)}, f32[128,1024]{1,0:T(8,128)}, f32[1,1024]{1,0:T(1,128)}, f32[16,1024]{1,0:T(8,128)}, /*index=5*/f32[1,1024]{1,0:T(1,128)}) custom-call(s32[4]{0:T(128)} %copy-done.29, f32[1280,128]{1,0:T(8,128)} %convert_add_fusion.6.refs_1_, ...), custom_call_target="tpu_custom_call" | custom-call | tf_op jit(solution)/shard_map/scan_backward/pallas_call | solution.py:261
  446.2 81.6 %scan_backward.3 = (f32[1280,128]{1,0:T(8,128)}, bf16[1024,1024]{1,0:T(8,128)(2,1)}, f32[128,1024]{1,0:T(8,128)}, f32[1,1024]{1,0:T(1,128)}, f32[16,1024]{1,0:T(8,128)}, /*index=5*/f32[1,1024]{1,0:T(1,128)}) custom-call(s32[4]{0:T(128)} %copy-done.29, f32[1280,128]{1,0:T(8,128)} %convert_add_fusion.5.refs_1_, ...), custom_call_target="tpu_custom_call" | custom-call | tf_op jit(solution)/shard_map/scan_backward/pallas_call | solution.py:261
  528.3 15.2 %fusion.33 = f32[2048,2048]{1,0:T(8,128)} fusion(bf16[2048,1024]{1,0:T(8,128)(2,1)} %get-tuple-element.181, bf16[2048,1024]{1,0:T(8,128)(2,1)} %all-gather.5.cloned.1.call-done), kind=kOutput, calls=%fused_computation.117 | convolution fusion | flops 8589934592 | bytes 25165824 | tf_op jit(solution)/shard_map/dot_general | solution.py:504
  545.9 8.4 %collective-permute-done.18 = bf16[1280,128]{1,0:T(8,128)(2,1)S(1)} collective-permute-done((bf16[1280,128]{1,0:T(8,128)(2,1)S(1)}, bf16[1280,128]{1,0:T(8,128)(2,1)S(1)}, u32[]{:S(2)}, u32[]{:S(2)}) %collective-permute-start.18) | collective-permute-done | bytes 327712 | tf_op jit(solution)/shard_map/ppermute | solution.py:453
  558.9 15.9 %conv_backward.2 = (bf16[2048,1024]{1,0:T(8,128)(2,1)}, f32[160,1024]{1,0:T(8,128)}, f32[1,1024]{1,0:T(1,128)}, f32[4,1024]{1,0:T(4,128)}) custom-call(s32[4]{0:T(128)} %copy-done.29, f32[1280,128]{1,0:T(8,128)} %convert_add_fusion.4.pg_ref, bf16[1024,1024]{1,0:T(8,128)(2,1)} %get-tuple-element.144.xg_ref, ...), custom_call_target="tpu_custom_call" | custom-call | tf_op jit(solution)/shard_map/conv_backward/pallas_call | solution.py:422
  575.7 15.7 %conv_backward.3 = (bf16[2048,1024]{1,0:T(8,128)(2,1)}, f32[160,1024]{1,0:T(8,128)}, f32[1,1024]{1,0:T(1,128)}, f32[4,1024]{1,0:T(4,128)}) custom-call(s32[4]{0:T(128)} %copy-done.29, f32[1280,128]{1,0:T(8,128)} %convert_add_fusion.3.pg_ref, bf16[1024,1024]{1,0:T(8,128)(2,1)} %get-tuple-element.141.xg_ref, ...), custom_call_target="tpu_custom_call", output_to_operand_aliasing={{0}: (9, {})} | custom-call | tf_op jit(solution)/shard_map/conv_backward/pallas_call | solution.py:422
  591.5 14.0 %fusion.34 = bf16[2048,1024]{1,0:T(8,128)(2,1)} fusion(bf16[2048,2048]{1,0:T(8,128)(2,1)} %get-tuple-element.121, bf16[2048,1024]{1,0:T(8,128)(2,1)} %get-tuple-element.162), kind=kOutput, calls=%fused_computation.118 | convolution fusion | flops 8589934592 | bytes 16777216 | tf_op jit(solution)/shard_map/dot_general | solution.py:504
  605.7 14.7 %add_convert_fusion = bf16[2048,2048]{1,0:T(8,128)(2,1)S(1)} fusion(f32[2048,2048]{1,0:T(8,128)} %fusion.33, bf16[2048,1024]{1,0:T(8,128)(2,1)} %get-tuple-element.162, bf16[2048,1024]{1,0:T(8,128)(2,1)} %bitcast.153), kind=kOutput, calls=%fused_computation | convolution fusion | flops 8598323200 | bytes 33554432 | tf_op jit(solution)/shard_map/dot_general | solution.py:504
  642.3 13.2 %collective-permute-done.23 = bf16[4,311,128]{2,1,0:T(8,128)(2,1)S(1)} collective-permute-done((bf16[4,311,128]{2,1,0:T(8,128)(2,1)S(1)}, bf16[4,311,128]{2,1,0:T(8,128)(2,1)S(1)}, u32[]{:S(2)}, u32[]{:S(2)}) %collective-permute-start.23) | collective-permute-done | bytes 318496 | tf_op jit(solution)/shard_map/ppermute | solution.py:497
  667.6 20.1 %collective-permute-done.22 = bf16[2,256,2048]{2,1,0:T(8,128)(2,1)} collective-permute-done((bf16[2,256,2048]{2,1,0:T(8,128)(2,1)}, bf16[2,256,2048]{2,1,0:T(8,128)(2,1)}, u32[]{:S(2)}, u32[]{:S(2)}) %collective-permute-start.22) | collective-permute-done | bytes 2097184 | tf_op jit(solution)/shard_map/ppermute | solution.py:453
  (286 shorter events, 157.8 us)
Async XLA Ops:
  7.3 15.3 %collective-permute-start.6 = (bf16[64]{0:T(256)(128)(2,1)}, bf16[64]{0:T(256)(128)(2,1)S(1)}, u32[]{:S(2)}, u32[]{:S(2)}) collective-permute-start(bf16[64]{0:T(256)(128)(2,1)} %param.16), channel_id=1, source_target_pairs={{0,2},{1,3},{2,0},{3,1},{4,6},{5,7},{6,4},{7,5},{8,10},{9,11},{10,... | collective-permute-start | bytes 392 | tf_op jit(solution)/shard_map/ppermute | solution.py:453
  17.4 93.0 %all-gather.9.cloned.1.call-start = ((), (), s32[]{:S(2)}) async-start(), calls=%async_computation.12 | async-start | bytes 5455872 | tf_op jit(solution)/shard_map/all_gather | solution.py:538
  27.8 222.3 %all-gather.5.cloned.1.call-start = ((), (), s32[]{:S(2)}) async-start(), calls=%async_computation.7 | async-start | bytes 4718592 | tf_op jit(solution)/shard_map/all_gather | solution.py:544
  28.1 26.1 %collective-permute-start.3 = (bf16[256,2048]{1,0:T(8,128)(2,1)S(1)}, bf16[256,2048]{1,0:T(8,128)(2,1)S(1)}, u32[]{:S(2)}, u32[]{:S(2)}) collective-permute-start(bf16[256,2048]{1,0:T(8,128)(2,1)S(1)} %get-tuple-element.107.refs_1_), channel_id=1, source_target_pairs={{0,2},{1,3},{2,0},{3,1},{4,6},{5,7},{6,4},{7,5},{8,10},{9,11},{10,... | collective-permute-start | bytes 3145736 | tf_op jit(solution)/shard_map/ppermute | solution.py:453
  29.8 46.2 %collective-permute-start = (bf16[256,2048]{1,0:T(8,128)(2,1)S(1)}, bf16[256,2048]{1,0:T(8,128)(2,1)S(1)}, u32[]{:S(2)}, u32[]{:S(2)}) collective-permute-start(bf16[256,2048]{1,0:T(8,128)(2,1)S(1)} %get-tuple-element.94.refs_1_), channel_id=1, source_target_pairs={{0,2},{1,3},{2,0},{3,1},{4,6},{5,7},{6,4},{7,5},{8,10},{9,11},{10,... | collective-permute-start | bytes 3145736 | tf_op jit(solution)/shard_map/ppermute | solution.py:453
  30.2 45.8 %collective-permute-start.4 = (bf16[256,2048]{1,0:T(8,128)(2,1)S(1)}, bf16[256,2048]{1,0:T(8,128)(2,1)S(1)}, u32[]{:S(2)}, u32[]{:S(2)}) collective-permute-start(bf16[256,2048]{1,0:T(8,128)(2,1)S(1)} %get-tuple-element.107.refs_1_), channel_id=1, source_target_pairs={{0,1},{1,0},{2,3},{3,2},{4,5},{5,4},{6,7},{7,6},{8,9},{9,8},{10,11... | collective-permute-start | bytes 3145736 | tf_op jit(solution)/shard_map/ppermute | solution.py:453
  30.2 45.8 %collective-permute-start.1 = (bf16[256,2048]{1,0:T(8,128)(2,1)S(1)}, bf16[256,2048]{1,0:T(8,128)(2,1)S(1)}, u32[]{:S(2)}, u32[]{:S(2)}) collective-permute-start(bf16[256,2048]{1,0:T(8,128)(2,1)S(1)} %get-tuple-element.94.refs_1_), channel_id=1, source_target_pairs={{0,1},{1,0},{2,3},{3,2},{4,5},{5,4},{6,7},{7,6},{8,9},{9,8},{10,11... | collective-permute-start | bytes 3145736 | tf_op jit(solution)/shard_map/ppermute | solution.py:453
  54.2 21.8 %collective-permute-start.5 = (bf16[256,2048]{1,0:T(8,128)(2,1)S(1)}, bf16[256,2048]{1,0:T(8,128)(2,1)S(1)}, u32[]{:S(2)}, u32[]{:S(2)}) collective-permute-start(bf16[256,2048]{1,0:T(8,128)(2,1)S(1)} %collective-permute-done.3.refs_2_), channel_id=1, source_target_pairs={{0,1},{1,0},{2,3},{3,2},{4,5},{5,4},{6,7},{7,6},{8,9},{9,8},{10,11... | collective-permute-start | bytes 3145736 | tf_op jit(solution)/shard_map/ppermute | solution.py:453
  93.3 177.8 %all-gather.7.cloned.1.call-start = ((), (), s32[]{:S(2)}) async-start(), calls=%async_computation.8 | async-start | bytes 4718592 | tf_op jit(solution)/shard_map/all_gather | solution.py:545
  134.1 312.0 %reduce-scatter.4.cloned.1.call-start = ((), (), s32[]{:S(2)}) async-start(), calls=%async_computation.9 | async-start | bytes 4718592 | tf_op jit(solution)/shard_map/reduce_scatter | solution.py:591
  159.1 43.0 %collective-permute-start.11 = (bf16[1280,128]{1,0:T(8,128)(2,1)S(1)}, bf16[1280,128]{1,0:T(8,128)(2,1)S(1)}, u32[]{:S(2)}, u32[]{:S(2)}) collective-permute-start(bf16[1280,128]{1,0:T(8,128)(2,1)S(1)} %add_convert_fusion.5), channel_id=1, source_target_pairs={{0,2},{1,3},{2,0},{3,1},{4,6},{5,7},{6,4},{7,5},{8,10},{9,11},{10,... | collective-permute-start | bytes 983048 | tf_op jit(solution)/shard_map/ppermute | solution.py:453
  203.0 46.7 %collective-permute-start.12 = (bf16[2,256,2048]{2,1,0:T(8,128)(2,1)S(1)}, bf16[2,256,2048]{2,1,0:T(8,128)(2,1)}, u32[]{:S(2)}, u32[]{:S(2)}) collective-permute-start(bf16[2,256,2048]{2,1,0:T(8,128)(2,1)S(1)} %copy-done.8), channel_id=1, source_target_pairs={{0,2},{1,3},{2,0},{3,1},{4,6},{5,7},{6,4},{7,5},{8,10},{9,11},{10,... | collective-permute-start | bytes 6291464 | tf_op jit(solution)/shard_map/ppermute | solution.py:453
  249.6 14.9 %collective-permute-start.13 = (bf16[2,256,2048]{2,1,0:T(8,128)(2,1)S(1)}, bf16[2,256,2048]{2,1,0:T(8,128)(2,1)}, u32[]{:S(2)}, u32[]{:S(2)}) collective-permute-start(bf16[2,256,2048]{2,1,0:T(8,128)(2,1)S(1)} %copy-done.8), channel_id=1, source_target_pairs={{0,1},{1,0},{2,3},{3,2},{4,5},{5,4},{6,7},{7,6},{8,9},{9,8},{10,11... | collective-permute-start | bytes 6291464 | tf_op jit(solution)/shard_map/ppermute | solution.py:453
  249.6 14.9 %collective-permute-start.14 = (bf16[2,256,2048]{2,1,0:T(8,128)(2,1)}, bf16[2,256,2048]{2,1,0:T(8,128)(2,1)}, u32[]{:S(2)}, u32[]{:S(2)}) collective-permute-start(bf16[2,256,2048]{2,1,0:T(8,128)(2,1)} %collective-permute-done.12), channel_id=1, source_target_pairs={{0,1},{1,0},{2,3},{3,2},{4,5},{5,4},{6,7},{7,6},{8,9},{9,8},{10,11... | collective-permute-start | bytes 6291464 | tf_op jit(solution)/shard_map/ppermute | solution.py:453
  336.9 218.3 %reduce-scatter.6.cloned.1.call-start = ((), (), s32[]{:S(2)}) async-start(), calls=%async_computation.10 | async-start | bytes 4718592 | tf_op jit(solution)/shard_map/reduce_scatter | solution.py:592
  355.0 86.0 %collective-permute-start.16 = (bf16[2,256,2048]{2,1,0:T(8,128)(2,1)S(1)}, bf16[2,256,2048]{2,1,0:T(8,128)(2,1)}, u32[]{:S(2)}, u32[]{:S(2)}) collective-permute-start(bf16[2,256,2048]{2,1,0:T(8,128)(2,1)S(1)} %split.33), channel_id=1, source_target_pairs={{0,2},{1,3},{2,0},{3,1},{4,6},{5,7},{6,4},{7,5},{8,10},{9,11},{10,... | collective-permute-start | bytes 6291464 | tf_op jit(solution)/shard_map/ppermute | solution.py:453
  440.9 102.6 %collective-permute-start.17 = (f32[1280,128]{1,0:T(8,128)}, f32[1280,128]{1,0:T(8,128)S(1)}, u32[]{:S(2)}, u32[]{:S(2)}) collective-permute-start(f32[1280,128]{1,0:T(8,128)} %get-tuple-element.132), channel_id=1, source_target_pairs={{0,1},{1,0},{2,3},{3,2},{4,5},{5,4},{6,7},{7,6},{8,9},{9,8},{10,11... | collective-permute-start | bytes 1966088 | tf_op jit(solution)/shard_map/ppermute | solution.py:453
  527.8 16.6 %collective-permute-start.19 = (f32[1280,128]{1,0:T(8,128)}, f32[1280,128]{1,0:T(8,128)S(1)}, u32[]{:S(2)}, u32[]{:S(2)}) collective-permute-start(f32[1280,128]{1,0:T(8,128)} %get-tuple-element.138), channel_id=1, source_target_pairs={{0,1},{1,0},{2,3},{3,2},{4,5},{5,4},{6,7},{7,6},{8,9},{9,8},{10,11... | collective-permute-start | bytes 1966088 | tf_op jit(solution)/shard_map/ppermute | solution.py:453
  544.4 30.4 %collective-permute-start.20 = (bf16[1280,128]{1,0:T(8,128)(2,1)S(1)}, bf16[1280,128]{1,0:T(8,128)(2,1)S(1)}, u32[]{:S(2)}, u32[]{:S(2)}) collective-permute-start(bf16[1280,128]{1,0:T(8,128)(2,1)S(1)} %add_convert_fusion.3), channel_id=1, source_target_pairs={{0,2},{1,3},{2,0},{3,1},{4,6},{5,7},{6,4},{7,5},{8,10},{9,11},{10,... | collective-permute-start | bytes 983048 | tf_op jit(solution)/shard_map/ppermute | solution.py:453
  555.2 20.5 %all-to-all-start.2 = ((bf16[4,64,1024]{2,1,0:T(8,128)(2,1)}), bf16[4,64,1024]{2,1,0:T(8,128)(2,1)S(1)}, u32[]{:S(2)}, u32[]{:S(2)}) async-start(bf16[4,64,1024]{2,1,0:T(8,128)(2,1)} %bitcast.167), calls=%async_computation.4 | async-start | bytes 1048576 | tf_op jit(solution)/shard_map/all_to_all | solution.py:593
  558.7 137.2 %reduce-scatter.8.cloned.1.call-start = ((), (), s32[]{:S(2)}) async-start(), calls=%async_computation.11 | async-start | bytes 4718592 | tf_op jit(solution)/shard_map/reduce_scatter | solution.py:618
  639.5 48.1 %collective-permute-start.22 = (bf16[2,256,2048]{2,1,0:T(8,128)(2,1)}, bf16[2,256,2048]{2,1,0:T(8,128)(2,1)}, u32[]{:S(2)}, u32[]{:S(2)}) collective-permute-start(bf16[2,256,2048]{2,1,0:T(8,128)(2,1)} %split.37), channel_id=1, source_target_pairs={{0,2},{1,3},{2,0},{3,1},{4,6},{5,7},{6,4},{7,5},{8,10},{9,11},{10,... | collective-permute-start | bytes 6291464 | tf_op jit(solution)/shard_map/ppermute | solution.py:453
  641.4 14.2 %collective-permute-start.23 = (bf16[4,311,128]{2,1,0:T(8,128)(2,1)S(1)}, bf16[4,311,128]{2,1,0:T(8,128)(2,1)S(1)}, u32[]{:S(2)}, u32[]{:S(2)}) collective-permute-start(bf16[4,311,128]{2,1,0:T(8,128)(2,1)S(1)} %fusion.16), channel_id=1, source_target_pairs={{0,4},{4,0},{8,12},{12,8},{16,20},{20,16},{24,28},{28,24},{1,5},{5... | collective-permute-start | bytes 955400 | tf_op jit(solution)/shard_map/ppermute | solution.py:497
  697.7 14.8 %all-to-all-start.3 = ((bf16[4,64,1024]{2,1,0:T(8,128)(2,1)}), bf16[4,64,1024]{2,1,0:T(8,128)(2,1)}, u32[]{:S(2)}, u32[]{:S(2)}) async-start(bf16[4,64,1024]{2,1,0:T(8,128)(2,1)} %bitcast.166), calls=%async_computation.6 | async-start | bytes 1048576 | tf_op jit(solution)/shard_map/all_to_all | solution.py:629
  (66 other events, 1081.1 us)
Sparse Core Ops, SparseCore 0:
  27.9 82.3 all-gather.8
  112.4 71.0 all-gather.4
  185.7 71.3 all-gather.6
  337.0 86.8 reduce-scatter.3
  427.4 87.9 reduce-scatter.5
  605.8 90.0 reduce-scatter.7
